TPU v7x, 768 devices: a whole 4x8x12 slice. The times are simulated.
768 devices in a mesh: row: 96 (over y_hi, z, core), col: 8 (over y_lo, x).
Axes of the slice: x: 4, y: 8 (y_hi: 4, y_lo: 2; y = y_hi * 2 + y_lo), z: 12, core: 2. Of those that a mesh axis runs over, the one named last changes fastest.
Arguments:
- raw_amps: float32 [24576, 3072], P('row', 'col'), may hold values from -24 to 24
- integrals: float32 [3072, 4096], P('row', 'col'), may hold values from -0.109375 to 0.109375
- occ_energy: float32 [256], replicated, may hold values from -2 to -0.5
- vir_energy: float32 [2048], replicated, may hold values from 0.5 to 3
- occ_pairs: int32 [24576, 2], P('row'), may hold values from 0 to 255
- vir_pairs: int32 [3072, 2], replicated, may hold values from 0 to 2047
- pair_order: int32 [3072], replicated, may hold values from 0 to 3071, each once
Outputs:
- residual: float32 [24576, 4096], P('row', 'col')
Inputs may be any that keep to these rules, and one draw needn't show every extreme that they name: `pair_order`: each column index appears exactly once.
All inputs are finite; a program needn't handle non-finite values.
Results may differ from a plain program's by a relative error of at most 0.000068.
Values sent between devices are 32-bit elements; how exact they have to be, the bound alone decides.
A program may use at most 64 MiB of HBM per device.

v0:
```python
import jax
import jax.numpy as jnp
from jax import lax
from jax.sharding import PartitionSpec as P


def on_device(raw_amps, integrals, occ_energy, vir_energy, occ_pairs, vir_pairs, pair_order):
    width = raw_amps.shape[1]
    col_start = lax.axis_index("col") * width
    local_pairs = lax.dynamic_slice_in_dim(vir_pairs, col_start, width, 0)
    occ_sum = occ_energy[occ_pairs[:, 0]] + occ_energy[occ_pairs[:, 1]]
    vir_sum = vir_energy[local_pairs[:, 0]] + vir_energy[local_pairs[:, 1]]
    scaled = raw_amps / (vir_sum[None, :] - occ_sum[:, None])
    gathered = lax.all_gather(scaled, "col", axis=1, tiled=True)
    ordered = jnp.take(gathered, pair_order, axis=1)
    return jnp.dot(
        ordered,
        lax.all_gather(integrals, "row", axis=0, tiled=True),
        preferred_element_type=jnp.float32,
        precision=lax.Precision.HIGHEST,
    )


def solution(mesh):
    placed = (P("row", "col"), P("row", "col"), P(), P(), P("row", None), P(), P())
    return jax.shard_map(
        on_device, mesh=mesh, in_specs=placed, out_specs=P("row", "col"), check_vma=False
    )
```

profile of v0, /device:TPU:1, one launch (start us, length us, event | category | flops | bytes accessed | tf_op | source)
XLA Modules:
  0.0 222.9 jit_solution(17702394637906417731)
XLA Ops:
  6.5 0.0 copy-start
  6.5 0.0 copy-start.1
  6.5 0.0 all-gather.3.cloned.1.call-start
  6.6 0.9 fusion.6
  7.4 0.0 copy-done
  7.4 0.0 copy-start.2
  7.4 2.5 %gather_fusion = f32[384]{0:T(512)S(1)} fusion(f32[2048]{0:T(1024)S(1)} %copy-done, s32[1024]{0:T(1024)S(1)} %get-tuple-element.10), kind=kCustom, calls=%fused_computation | custom fusion | bytes 4608 | tf_op jit(solution)/shard_map/gather | solution.py:12
  10.0 0.0 copy-start.3
  10.0 2.5 %gather_fusion.1 = f32[384]{0:T(512)S(1)} fusion(f32[2048]{0:T(1024)S(1)} %copy-done, s32[1024]{0:T(1024)S(1)} %get-tuple-element.9), kind=kCustom, calls=%fused_computation.1 | custom fusion | bytes 4608 | tf_op jit(solution)/shard_map/gather | solution.py:12
  12.5 0.0 copy-done.4
  12.6 0.0 copy-done.1
  12.6 1.9 gather_fusion.2
  14.6 1.9 gather_fusion.3
  16.5 0.0 copy-done.2
  16.5 0.2 copy.9
  16.7 0.9 subtract_divide_fusion
  17.6 0.0 all-gather.3.cloned.1.call-update
  17.6 0.0 all-gather.5.cloned.1.call-start
  17.7 0.7 all-gather.5.cloned.1.call-update
  18.4 0.0 copy-done.3
  18.4 56.5 %all-gather.3.cloned.1.call-done = f32[256,3072]{0,1:T(8,128)} async-done(((f32[256,384]{0,1:T(8,128)}), f32[256,3072]{0,1:T(8,128)}) %all-gather.3.cloned.1.call-update) | async-done | bytes 3145744 | tf_op jit(solution)/shard_map/all_gather | solution.py:14
  74.9 11.7 %gather_fusion.4 = f32[3072,256]{1,0:T(8,128)S(1)} fusion(f32[256,3072]{0,1:T(8,128)} %all-gather.3.cloned.1.call-done, s32[3072]{0:T(1024)S(1)} %fusion.4), kind=kCustom, calls=%fused_computation.4 | custom fusion | bytes 6303744 | tf_op jit(solution)/shard_map/jit(_take)/gather | solution.py:15
  86.6 119.9 %all-gather.5.cloned.1.call-done = f32[3072,512]{1,0:T(8,128)} async-done(((f32[32,512]{1,0:T(8,128)}), f32[3072,512]{1,0:T(8,128)}) %all-gather.5.cloned.1.call-update) | async-done | bytes 6291472 | tf_op jit(solution)/shard_map/all_gather | solution.py:18
  206.5 9.6 %fusion = f32[256,512]{1,0:T(8,128)} fusion(f32[3072,512]{1,0:T(8,128)} %all-gather.5.cloned.1.call-done, f32[3072,256]{1,0:T(8,128)S(1)} %gather_fusion.4, pred[3072]{0:T(1024)(128)(4,1)S(1)} %compare_and_fusion), kind=kOutput, calls=%fused_computation.5 | convolution fusion | flops 4832624640 | bytes 9964544 | tf_op jit(solution)/shard_map/dot_general | solution.py:16
  (9 shorter events, 0.1 us)
Async XLA Ops:
  6.5 0.9 copy-start
  6.5 6.0 %copy-start.4 = (s32[256,2]{0,1:T(2,128)S(1)}, s32[256,2]{0,1:T(2,128)}, u32[]{:S(2)}) copy-start(s32[256,2]{0,1:T(2,128)} %param.11) | copy-start | bytes 6148
  6.5 6.1 %copy-start.1 = (f32[256]{0:T(256)S(1)}, f32[256]{0:T(256)}, u32[]{:S(2)}) copy-start(f32[256]{0:T(256)} %param.9) | copy-start | bytes 3076
  6.5 68.4 %all-gather.3.cloned.1.call-start = ((), (), s32[]{:S(2)}) async-start(), calls=%async_computation | async-start | bytes 3538944 | tf_op jit(solution)/shard_map/all_gather | solution.py:14
  7.4 9.1 %copy-start.2 = (f32[256,384]{1,0:T(8,128)S(1)}, f32[256,384]{1,0:T(8,128)}, u32[]{:S(2)}) copy-start(f32[256,384]{1,0:T(8,128)} %param.7) | copy-start | bytes 1179652
  10.0 8.4 %copy-start.3 = (s32[3072]{0:T(1024)S(1)}, s32[3072]{0:T(1024)}, u32[]{:S(2)}) copy-start(s32[3072]{0:T(1024)} %param.13) | copy-start | bytes 36868
  17.6 188.9 %all-gather.5.cloned.1.call-start = ((), (), s32[]{:S(2)}) async-start(), calls=%async_computation.1 | async-start | bytes 6356992 | tf_op jit(solution)/shard_map/all_gather | solution.py:18
Sparse Core Ops, SparseCore 0:
  17.7 57.1 all-gather.2
  78.6 127.8 all-gather.4
where the time goes:
time: 223 us
  waiting for transfers between devices  177 us (79%)
  local copies, waits for them, and re-layouts  20.9 us (9%)
  between operations  13.6 us (6%)
  matrix products  9.6 us (4%)
    all_gather x1, waiting for transfers between devices, on_device(): lax.all_gather(integrals, 'row', axis=0, tiled=True)  120 us
    all_gather x1, waiting for transfers between devices, on_device(): gathered = lax.all_gather(scaled, 'col', axis=1, tiled=True)  56.5 us
    gather x1, local copies, waits for them, and re-layouts, on_device(): ordered = jnp.take(gathered, pair_order, axis=1)  11.7 us
    dot_general x1, matrix products, on_device(): jnp.dot(ordered, lax.all_gather(integrals, 'row', axis=0, tiled=True), pr...  9.6 us
    gather x2, local copies, waits for them, and re-layouts, on_device(): vir_sum = vir_energy[local_pairs[:, 0]] + vir_energy[local_pairs[:, 1]]  5.07 us
  transfers between devices with their start and end apart: 2, of which 2 were waited for; matrix products, arithmetic and copies ran while one was open for 5% of the time, Pallas kernels for 0%

commit v1 on v0

v1 whole, which is shorter than its diff:
```python
import functools

import jax
import jax.numpy as jnp
from jax import lax
from jax.experimental import pallas as pl
from jax.experimental.pallas import tpu as pltpu
from jax.sharding import PartitionSpec as P

MESH = pl.DeviceIdType.MESH
F32, BF16 = jnp.float32, jnp.bfloat16
NX, NYH, NZ = 4, 4, 12
ROWS, WIDTH, DEPTH, COLS = 256, 384, 32, 512
K = 3072
OFFSETS = (0, NYH - 1, 1, 2)
LAST = ((0, 1), (2, 3))


def kernel(
    raw, integ, occ_e, occ_p, vir_e, vir_p, order, out,
    amps, ints, pick, parts, moved, vir_sum, occ_sum,
    rz, ry, rs, ra, sz, sy, ss, sa, local,
):
    row, col = lax.axis_index("row"), lax.axis_index("col")
    core, z, yh = row % 2, (row // 2) % NZ, row // (2 * NZ)
    x, yl = col % NX, col // NX

    def device(x, yl, yh, z, core):
        return ((yh * NZ + z) * 2 + core, yl * NX + x)

    up, down = device(x, yl, yh, (z + 1) % NZ, core), device(x, yl, yh, (z + NZ - 1) % NZ, core)
    north, south = device(x, yl, (yh + 1) % NYH, z, core), device(x, yl, (yh + NYH - 1) % NYH, z, core)
    east, west = device((x + 1) % NX, yl, yh, z, core), device((x + NX - 1) % NX, yl, yh, z, core)
    partner, sibling = device(x, 1 - yl, yh, z, core), device(x, yl, yh, z, 1 - core)
    along_z = (up, down)

    def slot(z, core, yh):
        return z * 8 + core * 4 + yh

    def send(src, dst, ssem, rsem, to):
        pltpu.make_async_remote_copy(
            src_ref=src, dst_ref=dst, send_sem=ssem, recv_sem=rsem, device_id=to, device_id_type=MESH
        ).start()

    def wait(ref, sem):
        pltpu.make_async_copy(ref, ref, sem).wait()

    barrier = pltpu.get_barrier_semaphore()
    for to in (up, down, north, south, east, west, partner, sibling):
        pl.semaphore_signal(barrier, inc=1, device_id=to, device_id_type=MESH)
    pl.semaphore_wait(barrier, 8)

    own = slot(z, core, yh)
    mine = ints.at[own]
    send(integ, mine, sy.at[0], ry.at[0], north)
    send(integ, mine, sy.at[1], ry.at[1], south)
    send(integ, mine, sz.at[0], rz.at[0, 0, 0], up)
    send(integ, mine, sz.at[1], rz.at[1, 0, 0], down)
    g0, g1 = yl * NX, (1 - yl) * NX
    x_w, x_e, x_o = (x + NX - 1) % NX, (x + 1) % NX, (x + 2) % NX

    def half(block, h):
        return amps.at[block, pl.ds(h * (ROWS // 2), ROWS // 2)]

    for h in range(2):
        src = raw.at[pl.ds(h * (ROWS // 2), ROWS // 2)]
        send(src, half(col, h), sa.at[0], ra.at[0, h], east)
        send(src, half(col, h), sa.at[1], ra.at[1, h], west)
        send(src, half(col, h), sa.at[2], ra.at[2, h], partner)
    keep_b = pltpu.make_async_copy(integ, mine, local.at[0])
    keep_a = pltpu.make_async_copy(raw, amps.at[col], local.at[1])
    keep_b.start()
    keep_a.start()

    lane = lax.broadcasted_iota(jnp.int32, (ROWS, 256), 1)
    energy = jnp.broadcast_to(occ_e[...], (ROWS, 256))
    occ_sum[...] = jnp.sum(
        jnp.where(lane == occ_p[:, 0:1], energy, 0.0), axis=1, keepdims=True
    ) + jnp.sum(jnp.where(lane == occ_p[:, 1:2], energy, 0.0), axis=1, keepdims=True)
    table = vir_e[...]
    hi = table.astype(BF16)
    rest = table - hi.astype(F32)
    mid = rest.astype(BF16)
    low = (rest - mid.astype(F32)).astype(BF16)
    table = jnp.concatenate([hi, mid, low], axis=0)

    def vir_block(b, carry):
        total = jnp.zeros((1, WIDTH), F32)
        for j in range(2):
            index = vir_p[pl.ds(j, 1), pl.ds(pl.multiple_of(b * WIDTH, 128), WIDTH)]
            major = index // 128
            minor = index - major * 128
            hot = jnp.where(lax.broadcasted_iota(jnp.int32, (128, WIDTH), 0) == minor, 1.0, 0.0).astype(BF16)
            found = jnp.dot(table, hot, preferred_element_type=F32)
            found = found[0:16] + found[16:32] + found[32:48]
            total += jnp.sum(
                jnp.where(lax.broadcasted_iota(jnp.int32, (16, WIDTH), 0) == major, found, 0.0), axis=0, keepdims=True
            )
        vir_sum[b] = total
        return carry

    lax.fori_loop(0, 8, vir_block, 0)

    def fill(part):
        def some(i, carry):
            at = pl.multiple_of((part * 12 + i) * 64, 64)
            hot = lax.broadcasted_iota(jnp.int32, (64, K), 0) + at == order[...]
            pick[pl.ds(at, 64), :] = jnp.where(hot, 1.0, 0.0).astype(BF16)
            return carry

        lax.fori_loop(0, 12, some, 0)

    def permute(block, first=False):
        scaled = amps[block] / (vir_sum[block] - occ_sum[...])
        hi = scaled.astype(BF16)
        parts[0:ROWS, :] = hi
        parts[ROWS:, :] = (scaled - hi.astype(F32)).astype(BF16)

        def some(i, carry):
            at = pl.ds(pl.multiple_of(i * 512, 512), 512)
            rows = pl.ds(pl.multiple_of(block * WIDTH, 128), WIDTH)
            new = jnp.dot(parts[...], pick[rows, at], preferred_element_type=F32).astype(BF16)
            moved[:, at] = new if first else moved[:, at] + new
            return carry

        lax.fori_loop(0, 6, some, 0)

    def contract(zs):
        rows = ints[pl.ds(zs * 8, 8)].reshape(256, COLS)
        hi = rows.astype(BF16)
        low = (rows - hi.astype(F32)).astype(BF16)
        at = pl.ds(pl.multiple_of(zs * 256, 256), 256)
        a_hi, a_low = moved[0:ROWS, at], moved[ROWS:, at]
        out[...] += (
            jnp.dot(a_hi, hi, preferred_element_type=F32)
            + jnp.dot(a_low, hi, preferred_element_type=F32)
            + jnp.dot(a_hi, low, preferred_element_type=F32)
        )

    y_slots = [slot(z, core, (yh + off) % NYH) for off in OFFSETS]

    def plane(u):
        for way in range(2):
            send(ints.at[y_slots[u]], ints.at[y_slots[u]], sz.at[way], rz.at[way, 0, u], along_z[way])

    def piece(s, h):
        return ints.at[s, pl.ds(h * 16, 16)]

    wait(ints.at[own], ry.at[0])
    send(piece(y_slots[1], 0), piece(y_slots[1], 0), sy.at[2], ry.at[2], north)
    plane(1)
    wait(ints.at[own], ry.at[1])
    send(piece(y_slots[2], 1), piece(y_slots[2], 1), sy.at[3], ry.at[3], south)
    plane(2)

    def group(z, core):
        return ints.at[pl.ds(slot(z, core, 0), 4)]

    def to_sibling(z_from, index):
        send(group(z_from, core), group(z_from, core), ss, rs.at[index], sibling)

    def hop(t, u):
        for way in range(2):
            if t == 6 and u not in LAST[way]:
                continue
            z_from = (z + (NZ - t, t)[way]) % NZ
            s = slot(z_from, core, (yh + OFFSETS[u]) % NYH)
            wait(ints.at[s], rz.at[way, t - 1, u])
            if t < 5 or t == 5 and u in LAST[way]:
                send(ints.at[s], ints.at[s], sz.at[way], rz.at[way, t, u], along_z[way])
            if u == 3 and t < 6:
                to_sibling(z_from, 2 * t - 1 + way)

    def amps_in(index, block, h, then=()):
        wait(half(block, h), ra.at[index, h])
        for way, to_index in then:
            send(half(block, h), half(block, h), sa.at[way], ra.at[to_index, h], (east, west)[way])

    fill(0)
    wait(piece(own, 0), ry.at[2])
    wait(piece(own, 1), ry.at[3])
    plane(3)
    keep_b.wait()
    to_sibling(z, 0)
    keep_a.wait()
    hop(1, 0)
    fill(1)
    hop(1, 1)
    amps_in(0, g0 + x_w, 0, [(0, 3)])
    amps_in(2, g1 + x, 0, [(0, 4), (1, 5)])
    fill(2)
    hop(1, 2)
    fill(3)
    hop(1, 3)
    hop(2, 0)
    permute(col, True)
    hop(2, 1)
    amps_in(0, g0 + x_w, 1, [(0, 3)])
    amps_in(2, g1 + x, 1, [(0, 4), (1, 5)])
    hop(2, 2)
    permute(g0 + x_w)
    hop(2, 3)
    hop(3, 0)
    amps_in(1, g0 + x_e, 0)
    amps_in(1, g0 + x_e, 1)
    permute(g0 + x_e)
    hop(3, 1)
    amps_in(5, g1 + x_e, 0, [(1, 6)])
    hop(3, 2)
    permute(g1 + x)
    hop(3, 3)
    hop(4, 0)
    amps_in(5, g1 + x_e, 1, [(1, 6)])
    hop(4, 1)
    permute(g1 + x_e)
    hop(4, 2)
    amps_in(3, g0 + x_o, 0)
    amps_in(3, g0 + x_o, 1)
    permute(g0 + x_o)
    hop(4, 3)
    hop(5, 0)
    hop(5, 1)
    amps_in(4, g1 + x_w, 0)
    hop(5, 2)
    hop(5, 3)
    amps_in(4, g1 + x_w, 1)
    permute(g1 + x_w)
    for h in range(2):
        amps_in(6, g1 + x_o, h)
    permute(g1 + x_o)
    for i in range(11):
        wait(group(z, 0), rs.at[i])
    out[...] = jnp.zeros_like(out)

    def near(i, carry):
        contract((z + 7 + i) % NZ)
        return carry

    lax.fori_loop(0, 11, near, 0)
    for u in range(4):
        hop(6, u)
    z_far = (z + 6) % NZ
    to_sibling(z_far, 11)
    wait(group(z, 0), rs.at[11])
    contract(z_far)

    for way in range(2):
        wait(ints.at[pl.ds(0, 22)], sz.at[way])
        wait(ints.at[0], sy.at[way])
        wait(piece(0, 0), sy.at[2 + way])
        wait(amps.at[pl.ds(0, 3)], sa.at[way])
    wait(amps.at[0], sa.at[2])
    wait(ints.at[pl.ds(0, 48)], ss)


def on_device(raw_amps, integrals, occ_energy, vir_energy, occ_pairs, vir_pairs, pair_order):
    order = pair_order.reshape(NYH, NZ, 2, DEPTH).transpose(1, 2, 0, 3).reshape(1, K)
    vmem = pl.BlockSpec(memory_space=pltpu.VMEM)
    hbm = pl.BlockSpec(memory_space=pl.ANY)
    dma = pltpu.SemaphoreType.DMA
    return pl.pallas_call(
        kernel,
        out_shape=jax.ShapeDtypeStruct((ROWS, COLS), F32),
        in_specs=[hbm, hbm] + [vmem] * 5,
        out_specs=vmem,
        scratch_shapes=[
            pltpu.VMEM((8, ROWS, WIDTH), F32),
            pltpu.VMEM((96, DEPTH, COLS), F32),
            pltpu.VMEM((K, K), BF16),
            pltpu.VMEM((2 * ROWS, WIDTH), BF16),
            pltpu.VMEM((2 * ROWS, K), BF16),
            pltpu.VMEM((8, 1, WIDTH), F32),
            pltpu.VMEM((ROWS, 1), F32),
            dma((2, 6, 4)),
            dma((4,)),
            dma((12,)),
            dma((7, 2)),
            dma((2,)),
            dma((4,)),
            dma(()),
            dma((3,)),
            dma((2,)),
        ],
        compiler_params=pltpu.CompilerParams(
            collective_id=0, has_side_effects=True, vmem_limit_bytes=56 << 20
        ),
    )(
        raw_amps,
        integrals,
        occ_energy.reshape(1, 256),
        occ_pairs,
        vir_energy.reshape(16, 128),
        vir_pairs.T,
        order,
    )


def solution(mesh):
    placed = (P("row", "col"), P("row", "col"), P(), P(), P("row", None), P(), P())
    return jax.shard_map(
        on_device, mesh=mesh, in_specs=placed, out_specs=P("row", "col"), check_vma=False
    )
```

time: 223 us -> 80.4 us (0.36)
  waiting for transfers between devices: 177 us -> 0 us
  Pallas kernels: 0 us -> 76 us
  local copies, waits for them, and re-layouts: 20.9 us -> 4.18 us
  between operations: 13.6 us -> 0.03 us
  matrix products: 9.6 us -> 0 us
    all_gather x2 -> x0, waiting for transfers between devices: 176 us -> none  [the longest x1 120 us: on_device(): lax.all_gather(integrals, 'row', axis=0, tiled=True)]
    pallas_call x0 -> x1, Pallas kernels: none -> 76 us  [on_device(): pl.pallas_call(kernel, out_shape=jax.ShapeDtypeStruct((ROWS, COLS), F32),...]
    gather x5 -> x0, local copies, waits for them, and re-layouts: 20.7 us -> none  [the longest x1 11.7 us: on_device(): ordered = jnp.take(gathered, pair_order, axis=1)]
    dot_general x1 -> x0, matrix products: 9.6 us -> none  [on_device(): jnp.dot(ordered, lax.all_gather(integrals, 'row', axis=0, tiled=True), pr...]
    unnamed x11 -> x4, local copies, waits for them, and re-layouts: 0.19 us -> 2.68 us
  transfers between devices with their start and end apart: 2 -> 0, of which waited for: 2 -> 0; matrix products, arithmetic and copies ran while one was open for 5% -> 0% of each run, Pallas kernels for 0% -> 0%
where the time goes in v1:
time: 80.4 us; the launch traced here: 80.2 us
  Pallas kernels  76 us (95%)
  local copies, waits for them, and re-layouts  4.18 us (5%)
    pallas_call x1, Pallas kernels, on_device(): pl.pallas_call(kernel, out_shape=jax.ShapeDtypeStruct((ROWS, COLS), F32),...  76 us
    unnamed x4, local copies, waits for them, and re-layouts  2.68 us

profile of v1, /device:TPU:1, one launch (start us, length us, event | category | flops | bytes accessed | tf_op | source)
XLA Modules:
  0.0 80.2 jit_solution(15702513752534058199)
XLA Ops:
  0.0 0.8 reshape.14
  0.8 0.0 copy-start
  0.8 0.7 reshape.15.order
  1.5 0.0 copy-done
  1.5 0.8 copy.10.occ_p
  2.3 76.0 %shard_map.73 = f32[256,512]{1,0:T(8,128)} custom-call(f32[256,384]{1,0:T(8,128)} %raw.1, f32[32,512]{1,0:T(8,128)} %integ.1, f32[1,256]{1,0:T(1,128)} %bitcast.7, s32[256,2]{1,0:T(8,128)} %copy.10.occ_p, f32[16,128]{1,0:T(8,128)} %bitcast.6, s32[2,3072]{1,0:T(2,128)} %bitcast.5, s32[1,3072]{1,0:T(1,128)} %reshape.15.order), custom_call_target="tpu_custom_call" | custom-call | tf_op jit(solution)/shard_map/pallas_call | solution.py:261
  78.3 1.9 %copy.12 = f32[256,512]{1,0:T(8,128)} copy(f32[256,512]{1,0:T(8,128)} %shard_map.73) | data formatting | bytes 1048576
  (1 shorter events, 0.0 us)
Async XLA Ops:
  0.8 0.7 copy-start

commit v2 on v1

v2 whole, which is shorter than its diff:
```python
import functools

import jax
import jax.numpy as jnp
from jax import lax
from jax.experimental import pallas as pl
from jax.experimental.pallas import tpu as pltpu
from jax.sharding import PartitionSpec as P

MESH = pl.DeviceIdType.MESH
F32, BF16 = jnp.float32, jnp.bfloat16
NX, NYH, NZ = 4, 4, 12
ROWS, WIDTH, DEPTH, COLS = 256, 384, 32, 512
K = 3072
OFFSETS = (0, NYH - 1, 1, 2)
def kernel(
    raw, integ, occ_e, occ_p, vir_e, vir_p, order, out,
    amps, ints, pick, parts, moved, vir_sum, occ_sum, turned, place,
    rz, ry, rs, ra, rf, sz, sy, ss, sa, sf, local,
):
    row, col = lax.axis_index("row"), lax.axis_index("col")
    core, z, yh = row % 2, (row // 2) % NZ, row // (2 * NZ)
    x, yl = col % NX, col // NX

    def device(x, yl, yh, z, core):
        return ((yh * NZ + z) * 2 + core, yl * NX + x)

    up, down = device(x, yl, yh, (z + 1) % NZ, core), device(x, yl, yh, (z + NZ - 1) % NZ, core)
    north, south = device(x, yl, (yh + 1) % NYH, z, core), device(x, yl, (yh + NYH - 1) % NYH, z, core)
    east, west = device((x + 1) % NX, yl, yh, z, core), device((x + NX - 1) % NX, yl, yh, z, core)
    partner, sibling = device(x, 1 - yl, yh, z, core), device(x, yl, yh, z, 1 - core)
    along_z = (up, down)

    def slot(z, core, yh):
        return z * 8 + core * 4 + yh

    def send(src, dst, ssem, rsem, to):
        pltpu.make_async_remote_copy(
            src_ref=src, dst_ref=dst, send_sem=ssem, recv_sem=rsem, device_id=to, device_id_type=MESH
        ).start()

    def wait(ref, sem):
        pltpu.make_async_copy(ref, ref, sem).wait()

    barrier = pltpu.get_barrier_semaphore()
    for to in (up, down, north, south, east, west, partner, sibling):
        pl.semaphore_signal(barrier, inc=1, device_id=to, device_id_type=MESH)
    pl.semaphore_wait(barrier, 8)

    own = slot(z, core, yh)
    mine = ints.at[own]
    send(integ, mine, sy.at[0], ry.at[0], north)
    send(integ, mine, sy.at[1], ry.at[1], south)
    send(integ, mine, sz.at[0], rz.at[0, 0, 0], up)
    send(integ, mine, sz.at[1], rz.at[1, 0, 0], down)
    g0, g1 = yl * NX, (1 - yl) * NX
    x_w, x_e, x_o = (x + NX - 1) % NX, (x + 1) % NX, (x + 2) % NX

    def half(block, h):
        return amps.at[block, pl.ds(h * (ROWS // 2), ROWS // 2)]

    for h in range(2):
        for way, to in ((0, east), (1, west)):
            g = (h, 1 - h)[way]
            send(raw.at[pl.ds(g * (ROWS // 2), ROWS // 2)], half(col, g), sa.at[way], ra.at[way, g], to)
    keep_b = pltpu.make_async_copy(integ, mine, local.at[0])
    keep_a = pltpu.make_async_copy(raw, amps.at[col], local.at[1])
    keep_b.start()
    keep_a.start()

    sub = lax.broadcasted_iota(jnp.int32, (ROWS, 256), 0)
    lane = lax.broadcasted_iota(jnp.int32, (ROWS, 256), 1)
    energy = jnp.broadcast_to(occ_e[...], (ROWS, 256))
    total = jnp.zeros((ROWS, 1), F32)
    for j in range(2):
        orbital = jnp.broadcast_to(occ_p[j : j + 1, :].astype(F32), (ROWS, 256))
        orbital = jnp.sum(jnp.where(sub == lane, orbital, 0.0), axis=1, keepdims=True)
        total += jnp.sum(jnp.where(lane.astype(F32) == orbital, energy, 0.0), axis=1, keepdims=True)
    occ_sum[...] = total

    for shift in range(4):
        turned[shift] = order[...] if shift == 0 else pltpu.roll(order[...], shift * 32, 1)
    quarter = lax.broadcasted_iota(jnp.int32, (1, 128), 1) // 32
    for zs in range(NZ):
        for c in range(2):
            found = None
            for ys in range(NYH):
                here = turned[(ys - zs % 2 * 2 - c) % 4, pl.ds(ys * 6 + zs // 2, 1), :]
                found = here if found is None else jnp.where(quarter == ys, here, found)
            place[:, pl.ds(zs * 256 + c * 128, 128)] = found

    table = vir_e[...]
    hi = table.astype(BF16)
    rest = table - hi.astype(F32)
    mid = rest.astype(BF16)
    low = (rest - mid.astype(F32)).astype(BF16)
    table = jnp.concatenate([hi, mid, low], axis=0)

    def vir_block(b, carry):
        total = jnp.zeros((1, WIDTH), F32)
        for j in range(2):
            index = vir_p[pl.ds(j, 1), pl.ds(pl.multiple_of(b * WIDTH, 128), WIDTH)]
            major = index // 128
            minor = index - major * 128
            hot = jnp.where(lax.broadcasted_iota(jnp.int32, (128, WIDTH), 0) == minor, 1.0, 0.0).astype(BF16)
            found = jnp.dot(table, hot, preferred_element_type=F32)
            found = found[0:16] + found[16:32] + found[32:48]
            total += jnp.sum(
                jnp.where(lax.broadcasted_iota(jnp.int32, (16, WIDTH), 0) == major, found, 0.0), axis=0, keepdims=True
            )
        vir_sum[b] = total
        return carry

    blocks = [col, g0 + x_w, g0 + x_e, g1 + x, g0 + x_o, g1 + x_e, g1 + x_w, g1 + x_o]

    def fill(p):
        def some(i, carry):
            hot = lax.broadcasted_iota(jnp.int32, (64, K), 0) + (blocks[p] * WIDTH + i * 64) == place[...]
            pick[pl.ds(pl.multiple_of(p * WIDTH + i * 64, 64), 64), :] = jnp.where(hot, 1.0, 0.0).astype(BF16)
            return carry

        lax.fori_loop(0, 6, some, 0)

    def scale(p):
        scaled = amps[blocks[p]] / (vir_sum[blocks[p]] - occ_sum[...])
        hi = scaled.astype(BF16)
        parts[0:ROWS, p * WIDTH : (p + 1) * WIDTH] = hi
        parts[ROWS:, p * WIDTH : (p + 1) * WIDTH] = (scaled - hi.astype(F32)).astype(BF16)

    def permute(p, count, events=()):
        def some(i, carry):
            at = pl.ds(pl.multiple_of(i * 1024, 1024), 1024)
            here = slice(p * WIDTH, (p + count) * WIDTH)
            new = jnp.dot(parts[:, here], pick[here, at], preferred_element_type=F32).astype(BF16)
            moved[:, at] = new if p == 0 else moved[:, at] + new
            for j, event in enumerate(events):
                pl.when(i == j)(event)
            return carry

        lax.fori_loop(0, 3, some, 0)

    def contract(zs):
        rows = ints[pl.ds(zs * 8, 8)].reshape(256, COLS)
        hi = rows.astype(BF16)
        low = (rows - hi.astype(F32)).astype(BF16)
        at = pl.ds(pl.multiple_of(zs * 256, 256), 256)
        a_hi, a_low = moved[0:ROWS, at], moved[ROWS:, at]
        out[...] += (
            jnp.dot(a_hi, hi, preferred_element_type=F32)
            + jnp.dot(a_low, hi, preferred_element_type=F32)
            + jnp.dot(a_hi, low, preferred_element_type=F32)
        )

    y_slots = [slot(z, core, (yh + off) % NYH) for off in OFFSETS]

    def plane(u):
        for way in range(2):
            send(ints.at[y_slots[u]], ints.at[y_slots[u]], sz.at[way], rz.at[way, 0, u], along_z[way])

    def piece(s, h):
        return ints.at[s, pl.ds(h * 16, 16)]

    def group(z, core):
        return ints.at[pl.ds(slot(z, core, 0), 4)]

    def to_sibling(z_from, index):
        send(group(z_from, core), group(z_from, core), ss, rs.at[index], sibling)

    def source(t, way):
        return (z + (NZ - t, t)[way]) % NZ

    def hop(t, u):
        for way in range(2):
            s = slot(source(t, way), core, (yh + OFFSETS[u]) % NYH)
            wait(ints.at[s], rz.at[way, t - 1, u])
            if t < 5:
                send(ints.at[s], ints.at[s], sz.at[way], rz.at[way, t, u], along_z[way])
            elif u == 0:
                send(piece(s, way), piece(s, way), sz.at[way], rz.at[way, 5, 0], along_z[way])
            if u == 3:
                to_sibling(source(t, way), 2 * t - 1 + way)

    def hops(*pairs):
        def event():
            for t, u in pairs:
                hop(t, u)

        return event

    def amps_in(index, p, h, then=()):
        block = blocks[p]
        wait(half(block, h), ra.at[index, h])
        for way, to_index in then:
            send(half(block, h), half(block, h), sa.at[way], ra.at[to_index, h], (east, west)[way])

    z_far = (z + 6) % NZ
    f_slots = [slot(z_far, core, (yh + off) % NYH) for off in OFFSETS]

    def far_in():
        for way in range(2):
            here = piece(f_slots[0], way)
            wait(here, rz.at[way, 5, 0])
            send(here, here, sf.at[0], rf.at[0, way], north)
            send(here, here, sf.at[1], rf.at[1, way], south)

    def far_on():
        for way in range(2):
            here = piece(f_slots[1 + way], way)
            wait(here, rf.at[way, way])
            send(here, here, sf.at[way], rf.at[2, way], (north, south)[way])

    def far_end():
        for way in range(2):
            wait(piece(f_slots[1 + way], 1 - way), rf.at[way, 1 - way])
            wait(piece(f_slots[3], way), rf.at[2, way])

    fill(0)
    fill(1)
    hop(1, 0)
    wait(ints.at[own], ry.at[0])
    send(piece(y_slots[1], 0), piece(y_slots[1], 0), sy.at[2], ry.at[2], north)
    plane(1)
    wait(ints.at[own], ry.at[1])
    send(piece(y_slots[2], 1), piece(y_slots[2], 1), sy.at[3], ry.at[3], south)
    plane(2)
    for h in range(2):
        send(raw.at[pl.ds(h * (ROWS // 2), ROWS // 2)], half(col, h), sa.at[2], ra.at[2, h], partner)
    lax.fori_loop(0, 8, vir_block, 0)
    amps_in(0, 1, 0, [(0, 3)])
    amps_in(1, 2, 1, [(1, 3)])
    hop(2, 0)
    wait(piece(own, 0), ry.at[2])
    wait(piece(own, 1), ry.at[3])
    plane(3)
    keep_b.wait()
    to_sibling(z, 0)
    fill(2)
    fill(3)
    hop(1, 1)
    keep_a.wait()
    scale(0)
    fill(4)
    hop(1, 2)

    def partner_in(h):
        amps_in(2, 3, h, [(0, 4), (1, 5)])

    permute(0, 1, [hops((3, 0)), hops((1, 3)), hops((2, 1))])
    partner_in(0)
    amps_in(0, 1, 1)
    amps_in(1, 2, 0)
    scale(1)
    scale(2)
    permute(1, 2, [hops((2, 2)), hops((4, 0)), hops((2, 3))])
    partner_in(1)
    fill(5)
    hop(3, 1)
    amps_in(3, 4, 0)
    amps_in(3, 4, 1)
    scale(3)
    scale(4)
    hop(3, 2)
    amps_in(4, 6, 0, [(0, 6)])
    permute(3, 2, [hops((5, 0)), hops((3, 3)), hops((4, 1))])
    amps_in(5, 5, 1, [(1, 6)])
    fill(6)
    hop(4, 2)
    fill(7)
    amps_in(4, 6, 1)
    amps_in(5, 5, 0)
    scale(5)
    scale(6)
    far_in()
    permute(5, 2, [hops((4, 3)), hops((5, 1))])
    far_on()
    for h in range(2):
        amps_in(6, 7, h)
    scale(7)
    permute(7, 1)
    hop(5, 2)
    hop(5, 3)
    for i in range(9):
        wait(group(z, 0), rs.at[i])
    out[...] = jnp.zeros_like(out)

    def near(i, carry):
        contract((z + 8 + i) % NZ)
        return carry

    lax.fori_loop(0, 9, near, 0)
    far_end()
    to_sibling(z_far, 11)
    for i in range(9, 11):
        wait(group(z, 0), rs.at[i])
    contract((z + 5) % NZ)
    contract((z + 7) % NZ)
    wait(group(z, 0), rs.at[11])
    contract(z_far)

    for way in range(2):
        wait(ints.at[pl.ds(0, 41), pl.ds(0, 16)], sz.at[way])
        wait(ints.at[0], sy.at[way])
        wait(piece(0, 0), sy.at[2 + way])
        wait(ints.at[pl.ds(0, 3), pl.ds(0, 16)], sf.at[way])
        wait(amps.at[pl.ds(0, 3)], sa.at[way])
    wait(amps.at[0], sa.at[2])
    wait(ints.at[pl.ds(0, 48)], ss)


def on_device(raw_amps, integrals, occ_energy, vir_energy, occ_pairs, vir_pairs, pair_order):
    vmem = pl.BlockSpec(memory_space=pltpu.VMEM)
    hbm = pl.BlockSpec(memory_space=pl.ANY)
    dma = pltpu.SemaphoreType.DMA
    return pl.pallas_call(
        kernel,
        out_shape=pltpu.VMEM((ROWS, COLS), F32),
        in_specs=[hbm, hbm] + [vmem] * 5,
        out_specs=vmem,
        scratch_shapes=[
            pltpu.VMEM((8, ROWS, WIDTH), F32),
            pltpu.VMEM((96, DEPTH, COLS), F32),
            pltpu.VMEM((K, K), BF16),
            pltpu.VMEM((2 * ROWS, K), BF16),
            pltpu.VMEM((2 * ROWS, K), BF16),
            pltpu.VMEM((8, 1, WIDTH), F32),
            pltpu.VMEM((ROWS, 1), F32),
            pltpu.VMEM((4, 24, 128), jnp.int32),
            pltpu.VMEM((1, K), jnp.int32),
            dma((2, 6, 4)),
            dma((4,)),
            dma((12,)),
            dma((7, 2)),
            dma((3, 2)),
            dma((2,)),
            dma((4,)),
            dma(()),
            dma((3,)),
            dma((2,)),
            dma((2,)),
        ],
        compiler_params=pltpu.CompilerParams(
            collective_id=0, has_side_effects=True, vmem_limit_bytes=56 << 20
        ),
    )(
        raw_amps,
        integrals,
        occ_energy.reshape(1, 256),
        occ_pairs.T,
        vir_energy.reshape(16, 128),
        vir_pairs.T,
        pair_order.reshape(24, 128),
    )


def solution(mesh):
    placed = (P("row", "col"), P("row", "col"), P(), P(), P("row", None), P(), P())
    return jax.shard_map(
        on_device, mesh=mesh, in_specs=placed, out_specs=P("row", "col"), check_vma=False
    )
```

time: 80.4 us -> 61.8 us (0.77)
  Pallas kernels: 76 us -> 60.8 us
  local copies, waits for them, and re-layouts: 4.18 us -> 0.8 us
    pallas_call x1, Pallas kernels: 76 us -> 60.8 us  [on_device(): pl.pallas_call(kernel, out_shape=pltpu.VMEM((ROWS, COLS), F32), in_specs=...]
    unnamed x4 -> x1, local copies, waits for them, and re-layouts: 2.68 us -> 0.8 us
    reshape x2 -> x0, local copies, waits for them, and re-layouts: 1.49 us -> none  [on_device(): pair_order.reshape(NYH, NZ, 2, DEPTH).transpose(1, 2, 0, 3).reshape(1, K)]
where the time goes in v2:
time: 61.8 us; the launch traced here: 61.6 us
  Pallas kernels  60.8 us (98%)
  local copies, waits for them, and re-layouts  0.8 us (1%)
    pallas_call x1, Pallas kernels, on_device(): pl.pallas_call(kernel, out_shape=pltpu.VMEM((ROWS, COLS), F32), in_specs=...  60.8 us

profile of v2, /device:TPU:1, one launch (start us, length us, event | category | flops | bytes accessed | tf_op | source)
XLA Modules:
  0.0 61.6 jit_solution(5244937184684269799)
XLA Ops:
  0.0 60.8 %shard_map.73 = f32[256,512]{1,0:T(8,128)S(1)} custom-call(f32[256,384]{1,0:T(8,128)} %raw.1, f32[32,512]{1,0:T(8,128)} %integ.1, f32[1,256]{1,0:T(1,128)} %bitcast.9, s32[2,256]{1,0:T(2,128)} %bitcast.8, f32[16,128]{1,0:T(8,128)} %bitcast.7, s32[2,3072]{1,0:T(2,128)} %bitcast.5, s32[24,128]{1,0:T(8,128)} %bitcast.6), custom_call_target="tpu_custom_call" | custom-call | tf_op jit(solution)/shard_map/pallas_call | solution.py:314
  60.8 0.8 %copy.9 = f32[256,512]{1,0:T(8,128)} copy(f32[256,512]{1,0:T(8,128)S(1)} %shard_map.73) | data formatting | bytes 1048576

commit v3 on v2

--- a/solution.py
+++ b/solution.py
@@ -16,7 +16,7 @@
 def kernel(
     raw, integ, occ_e, occ_p, vir_e, vir_p, order, out,
     amps, ints, pick, parts, moved, vir_sum, occ_sum, turned, place,
-    rz, ry, rs, ra, rf, sz, sy, ss, sa, sf, local,
+    rz, ry, rs, ra, rb, rf, sz, sy, ss, sa, sf, local,
 ):
     row, col = lax.axis_index("row"), lax.axis_index("col")
     core, z, yh = row % 2, (row // 2) % NZ, row // (2 * NZ)
@@ -28,6 +28,7 @@
     up, down = device(x, yl, yh, (z + 1) % NZ, core), device(x, yl, yh, (z + NZ - 1) % NZ, core)
     north, south = device(x, yl, (yh + 1) % NYH, z, core), device(x, yl, (yh + NYH - 1) % NYH, z, core)
     east, west = device((x + 1) % NX, yl, yh, z, core), device((x + NX - 1) % NX, yl, yh, z, core)
+    up2, down2 = device(x, yl, yh, (z + 2) % NZ, core), device(x, yl, yh, (z + NZ - 2) % NZ, core)
     partner, sibling = device(x, 1 - yl, yh, z, core), device(x, yl, yh, z, 1 - core)
     along_z = (up, down)
 
@@ -43,16 +44,20 @@
         pltpu.make_async_copy(ref, ref, sem).wait()
 
     barrier = pltpu.get_barrier_semaphore()
-    for to in (up, down, north, south, east, west, partner, sibling):
+    for to in (up, down, up2, down2, north, south, east, west, partner, sibling):
         pl.semaphore_signal(barrier, inc=1, device_id=to, device_id_type=MESH)
-    pl.semaphore_wait(barrier, 8)
+    pl.semaphore_wait(barrier, 10)
 
     own = slot(z, core, yh)
     mine = ints.at[own]
-    send(integ, mine, sy.at[0], ry.at[0], north)
-    send(integ, mine, sy.at[1], ry.at[1], south)
+    for h in range(2):
+        for way, to in ((0, north), (1, south)):
+            g = (h, 1 - h)[way]
+            send(integ.at[pl.ds(g * 16, 16)], ints.at[own, pl.ds(g * 16, 16)], sy.at[way], ry.at[way, g], to)
     send(integ, mine, sz.at[0], rz.at[0, 0, 0], up)
     send(integ, mine, sz.at[1], rz.at[1, 0, 0], down)
+    send(integ, mine, sz.at[0], rz.at[0, 1, 0], up2)
+    send(integ, mine, sz.at[1], rz.at[1, 1, 0], down2)
     g0, g1 = yl * NX, (1 - yl) * NX
     x_w, x_e, x_o = (x + NX - 1) % NX, (x + 1) % NX, (x + 2) % NX
 
@@ -61,8 +66,7 @@
 
     for h in range(2):
         for way, to in ((0, east), (1, west)):
-            g = (h, 1 - h)[way]
-            send(raw.at[pl.ds(g * (ROWS // 2), ROWS // 2)], half(col, g), sa.at[way], ra.at[way, g], to)
+            send(raw.at[pl.ds(h * (ROWS // 2), ROWS // 2)], half(col, h), sa.at[way], ra.at[way, h], to)
     keep_b = pltpu.make_async_copy(integ, mine, local.at[0])
     keep_a = pltpu.make_async_copy(raw, amps.at[col], local.at[1])
     keep_b.start()
@@ -139,12 +143,17 @@
 
         lax.fori_loop(0, 3, some, 0)
 
-    def contract(zs):
-        rows = ints[pl.ds(zs * 8, 8)].reshape(256, COLS)
+    def contract(chosen):
+        rows = jnp.concatenate(
+            [ints[pl.ds(z_from * 8 + first, n)].reshape(n * DEPTH, COLS) for z_from, first, n in chosen], axis=0
+        )
         hi = rows.astype(BF16)
         low = (rows - hi.astype(F32)).astype(BF16)
-        at = pl.ds(pl.multiple_of(zs * 256, 256), 256)
-        a_hi, a_low = moved[0:ROWS, at], moved[ROWS:, at]
+        at = [
+            pl.ds(pl.multiple_of(z_from * 256 + first * DEPTH, 128), n * DEPTH) for z_from, first, n in chosen
+        ]
+        a_hi = jnp.concatenate([moved[0:ROWS, cols] for cols in at], axis=1)
+        a_low = jnp.concatenate([moved[ROWS:, cols] for cols in at], axis=1)
         out[...] += (
             jnp.dot(a_hi, hi, preferred_element_type=F32)
             + jnp.dot(a_low, hi, preferred_element_type=F32)
@@ -153,9 +162,10 @@
 
     y_slots = [slot(z, core, (yh + off) % NYH) for off in OFFSETS]
 
-    def plane(u):
-        for way in range(2):
-            send(ints.at[y_slots[u]], ints.at[y_slots[u]], sz.at[way], rz.at[way, 0, u], along_z[way])
+    def plane(u, h):
+        here = piece(y_slots[u], h)
+        for way in range(2):
+            send(here, here, sz.at[way], rz.at[way, 0, u], along_z[way])
 
     def piece(s, h):
         return ints.at[s, pl.ds(h * 16, 16)]
@@ -169,29 +179,41 @@
     def source(t, way):
         return (z + (NZ - t, t)[way]) % NZ
 
+    def block_to_sibling(s, index):
+        send(ints.at[s], ints.at[s], ss, rs.at[index], sibling)
+
     def hop(t, u):
         for way in range(2):
             s = slot(source(t, way), core, (yh + OFFSETS[u]) % NYH)
             wait(ints.at[s], rz.at[way, t - 1, u])
-            if t < 5:
+            if t < 5 and (t, u) != (1, 0):
                 send(ints.at[s], ints.at[s], sz.at[way], rz.at[way, t, u], along_z[way])
-            elif u == 0:
+            elif t == 5 and u == 0:
                 send(piece(s, way), piece(s, way), sz.at[way], rz.at[way, 5, 0], along_z[way])
-            if u == 3:
+            if t == 5:
+                block_to_sibling(s, 9 + way)
+            elif u == 3:
                 to_sibling(source(t, way), 2 * t - 1 + way)
 
-    def hops(*pairs):
-        def event():
-            for t, u in pairs:
-                hop(t, u)
-
-        return event
-
-    def amps_in(index, p, h, then=()):
-        block = blocks[p]
-        wait(half(block, h), ra.at[index, h])
-        for way, to_index in then:
-            send(half(block, h), half(block, h), sa.at[way], ra.at[to_index, h], (east, west)[way])
+    def quarter_of(block, h, way):
+        return amps.at[block, pl.ds(h * (ROWS // 2) + way * (ROWS // 4), ROWS // 4)]
+
+    def amps_in(far, h):
+        for way, p in ((0, (1, 6)[far]), (1, (2, 5)[far])):
+            wait(half(blocks[p], h), ra.at[(0, 3)[far] + way, h])
+            here = quarter_of(blocks[p], h, way)
+            send(here, here, sa.at[way], rb.at[far, h, way], (east, west)[way])
+
+    def partner_in(h):
+        wait(half(blocks[3], h), ra.at[2, h])
+        for way in range(2):
+            here = half(blocks[3], h)
+            send(here, here, sa.at[way], ra.at[3 + way, h], (east, west)[way])
+
+    def opposite_in(far):
+        for h in range(2):
+            for way in range(2):
+                wait(quarter_of(blocks[(4, 7)[far]], h, way), rb.at[far, h, way])
 
     z_far = (z + 6) % NZ
     f_slots = [slot(z_far, core, (yh + off) % NYH) for off in OFFSETS]
@@ -213,89 +235,87 @@
         for way in range(2):
             wait(piece(f_slots[1 + way], 1 - way), rf.at[way, 1 - way])
             wait(piece(f_slots[3], way), rf.at[2, way])
-
+        to_sibling(z_far, 11)
+
+    def side_in(h, way):
+        wait(piece(y_slots[1 + way], h), ry.at[way, h])
+        if h == way:
+            send(piece(y_slots[1 + way], h), piece(y_slots[1 + way], h), sy.at[2 + way], ry.at[2, way], (north, south)[way])
+        plane(1 + way, h)
+
+    def steps(*calls):
+        def event():
+            for call, *args in calls:
+                call(*args)
+
+        return event
+
+    def plane_end():
+        for h in range(2):
+            wait(piece(y_slots[3], h), ry.at[2, h])
+            plane(3, h)
+        keep_b.wait()
+        to_sibling(z, 0)
+
+    lax.fori_loop(0, 8, vir_block, 0)
     fill(0)
     fill(1)
-    hop(1, 0)
-    wait(ints.at[own], ry.at[0])
-    send(piece(y_slots[1], 0), piece(y_slots[1], 0), sy.at[2], ry.at[2], north)
-    plane(1)
-    wait(ints.at[own], ry.at[1])
-    send(piece(y_slots[2], 1), piece(y_slots[2], 1), sy.at[3], ry.at[3], south)
-    plane(2)
+    keep_a.wait()
+    scale(0)
+    side_in(0, 0)
+    side_in(1, 1)
+    fill(2)
+    side_in(1, 0)
+    side_in(0, 1)
     for h in range(2):
         send(raw.at[pl.ds(h * (ROWS // 2), ROWS // 2)], half(col, h), sa.at[2], ra.at[2, h], partner)
-    lax.fori_loop(0, 8, vir_block, 0)
-    amps_in(0, 1, 0, [(0, 3)])
-    amps_in(1, 2, 1, [(1, 3)])
+    hop(1, 0)
     hop(2, 0)
-    wait(piece(own, 0), ry.at[2])
-    wait(piece(own, 1), ry.at[3])
-    plane(3)
-    keep_b.wait()
-    to_sibling(z, 0)
-    fill(2)
+    permute(0, 1, [steps((amps_in, 0, 0)), steps((plane_end,))])
     fill(3)
     hop(1, 1)
-    keep_a.wait()
-    scale(0)
     fill(4)
-    hop(1, 2)
-
-    def partner_in(h):
-        amps_in(2, 3, h, [(0, 4), (1, 5)])
-
-    permute(0, 1, [hops((3, 0)), hops((1, 3)), hops((2, 1))])
-    partner_in(0)
-    amps_in(0, 1, 1)
-    amps_in(1, 2, 0)
+    amps_in(0, 1)
+    hop(3, 0)
     scale(1)
     scale(2)
-    permute(1, 2, [hops((2, 2)), hops((4, 0)), hops((2, 3))])
+    hop(1, 2)
+    hop(1, 3)
+    partner_in(0)
+    permute(1, 2, [steps((hop, 2, 1)), steps((hop, 4, 0)), steps((hop, 2, 2))])
     partner_in(1)
     fill(5)
-    hop(3, 1)
-    amps_in(3, 4, 0)
-    amps_in(3, 4, 1)
+    hop(2, 3)
+    opposite_in(0)
     scale(3)
     scale(4)
-    hop(3, 2)
-    amps_in(4, 6, 0, [(0, 6)])
-    permute(3, 2, [hops((5, 0)), hops((3, 3)), hops((4, 1))])
-    amps_in(5, 5, 1, [(1, 6)])
-    fill(6)
-    hop(4, 2)
-    fill(7)
-    amps_in(4, 6, 1)
-    amps_in(5, 5, 0)
+    hop(5, 0)
+    hop(3, 1)
+    amps_in(1, 0)
+    permute(3, 2, [steps((hop, 3, 2)), steps((far_in,), (hop, 3, 3)), steps((amps_in, 1, 1))])
     scale(5)
     scale(6)
-    far_in()
-    permute(5, 2, [hops((4, 3)), hops((5, 1))])
-    far_on()
-    for h in range(2):
-        amps_in(6, 7, h)
+    hop(4, 1)
+    fill(6)
+    fill(7)
+    permute(5, 2, [steps((hop, 4, 2)), steps((hop, 4, 3)), steps((far_on,))])
+    opposite_in(1)
     scale(7)
-    permute(7, 1)
-    hop(5, 2)
-    hop(5, 3)
+    permute(7, 1, [steps((hop, 5, 1)), steps((hop, 5, 2)), steps((hop, 5, 3))])
     for i in range(9):
         wait(group(z, 0), rs.at[i])
     out[...] = jnp.zeros_like(out)
 
     def near(i, carry):
-        contract((z + 8 + i) % NZ)
+        contract([((z + 8 + i * 3 + j) % NZ, 0, 8) for j in range(3)])
+        pl.when(i == 0)(far_end)
         return carry
 
-    lax.fori_loop(0, 9, near, 0)
-    far_end()
-    to_sibling(z_far, 11)
-    for i in range(9, 11):
+    lax.fori_loop(0, 3, near, 0)
+    contract([(z_from, core * 4, 4) for z_from in ((z + 5) % NZ, z_far, (z + 7) % NZ)])
+    for i in range(9, 12):
         wait(group(z, 0), rs.at[i])
-    contract((z + 5) % NZ)
-    contract((z + 7) % NZ)
-    wait(group(z, 0), rs.at[11])
-    contract(z_far)
+    contract([(z_from, 4 - core * 4, 4) for z_from in ((z + 5) % NZ, z_far, (z + 7) % NZ)])
 
     for way in range(2):
         wait(ints.at[pl.ds(0, 41), pl.ds(0, 16)], sz.at[way])
@@ -327,9 +347,10 @@
             pltpu.VMEM((4, 24, 128), jnp.int32),
             pltpu.VMEM((1, K), jnp.int32),
             dma((2, 6, 4)),
-            dma((4,)),
+            dma((3, 2)),
             dma((12,)),
-            dma((7, 2)),
+            dma((5, 2)),
+            dma((2, 2, 2)),
             dma((3, 2)),
             dma((2,)),
             dma((4,)),

time: 61.8 us -> 58.4 us (0.945)
  Pallas kernels: 60.8 us -> 57.4 us
    pallas_call x1, Pallas kernels: 60.8 us -> 57.4 us  [on_device(): pl.pallas_call(kernel, out_shape=pltpu.VMEM((ROWS, COLS), F32), in_specs=...]
where the time goes in v3:
time: 58.4 us; the launch traced here: 58.2 us
  Pallas kernels  57.4 us (98%)
  local copies, waits for them, and re-layouts  0.8 us (1%)
    pallas_call x1, Pallas kernels, on_device(): pl.pallas_call(kernel, out_shape=pltpu.VMEM((ROWS, COLS), F32), in_specs=...  57.4 us

profile of v3, /device:TPU:1, one launch (start us, length us, event | category | flops | bytes accessed | tf_op | source)
XLA Modules:
  0.0 58.2 jit_solution(2526908048743147975)
XLA Ops:
  0.0 57.4 %shard_map.73 = f32[256,512]{1,0:T(8,128)S(1)} custom-call(f32[256,384]{1,0:T(8,128)} %raw.1, f32[32,512]{1,0:T(8,128)} %integ.1, f32[1,256]{1,0:T(1,128)} %bitcast.9, s32[2,256]{1,0:T(2,128)} %bitcast.8, f32[16,128]{1,0:T(8,128)} %bitcast.7, s32[2,3072]{1,0:T(2,128)} %bitcast.5, s32[24,128]{1,0:T(8,128)} %bitcast.6), custom_call_target="tpu_custom_call" | custom-call | tf_op jit(solution)/shard_map/pallas_call | solution.py:334
  57.4 0.8 %copy.9 = f32[256,512]{1,0:T(8,128)} copy(f32[256,512]{1,0:T(8,128)S(1)} %shard_map.73) | data formatting | bytes 1048576

commit v4 on v3

--- a/solution.py
+++ b/solution.py
@@ -16,7 +16,7 @@
 def kernel(
     raw, integ, occ_e, occ_p, vir_e, vir_p, order, out,
     amps, ints, pick, parts, moved, vir_sum, occ_sum, turned, place,
-    rz, ry, rs, ra, rb, rf, sz, sy, ss, sa, sf, local,
+    rz, rg, ry, rs, ra, rb, rf, sg, sz, sy, ss, sa, sf, local,
 ):
     row, col = lax.axis_index("row"), lax.axis_index("col")
     core, z, yh = row % 2, (row // 2) % NZ, row // (2 * NZ)
@@ -182,12 +182,29 @@
     def block_to_sibling(s, index):
         send(ints.at[s], ints.at[s], ss, rs.at[index], sibling)
 
+    def eighth(way, u, h):
+        return ints.at[slot(source(3, way), core, (yh + OFFSETS[u]) % NYH), pl.ds(h * 8, 8)]
+
+    def mid_on():
+        for way in range(2):
+            for side, to in ((0, north), (1, south)):
+                wait(piece(slot(source(3, way), core, (yh + OFFSETS[1 + side]) % NYH), 0), rg.at[way, side])
+                here = eighth(way, 1 + side, side)
+                send(here, here, sg.at[way, side], rg.at[way, 2 + side], to)
+
     def hop(t, u):
         for way in range(2):
             s = slot(source(t, way), core, (yh + OFFSETS[u]) % NYH)
-            wait(ints.at[s], rz.at[way, t - 1, u])
+            wait(piece(s, 1) if t == 3 and u else ints.at[s], rz.at[way, t - 1, u])
+            if t == 3 and u == 0:
+                for side, to in ((0, north), (1, south)):
+                    send(piece(s, 0), piece(s, 0), sg.at[way, side], rg.at[way, side], to)
+            if t == 3 and u == 3:
+                for side in range(2):
+                    wait(eighth(way, 3, side), rg.at[way, 2 + side])
             if t < 5 and (t, u) != (1, 0):
-                send(ints.at[s], ints.at[s], sz.at[way], rz.at[way, t, u], along_z[way])
+                here = piece(s, 1) if t == 2 and u else ints.at[s]
+                send(here, here, sz.at[way], rz.at[way, t, u], along_z[way])
             elif t == 5 and u == 0:
                 send(piece(s, way), piece(s, way), sz.at[way], rz.at[way, 5, 0], along_z[way])
             if t == 5:
@@ -264,11 +281,11 @@
     scale(0)
     side_in(0, 0)
     side_in(1, 1)
+    for h in range(2):
+        send(raw.at[pl.ds(h * (ROWS // 2), ROWS // 2)], half(col, h), sa.at[2], ra.at[2, h], partner)
     fill(2)
     side_in(1, 0)
     side_in(0, 1)
-    for h in range(2):
-        send(raw.at[pl.ds(h * (ROWS // 2), ROWS // 2)], half(col, h), sa.at[2], ra.at[2, h], partner)
     hop(1, 0)
     hop(2, 0)
     permute(0, 1, [steps((amps_in, 0, 0)), steps((plane_end,))])
@@ -290,6 +307,7 @@
     scale(3)
     scale(4)
     hop(5, 0)
+    mid_on()
     hop(3, 1)
     amps_in(1, 0)
     permute(3, 2, [steps((hop, 3, 2)), steps((far_in,), (hop, 3, 3)), steps((amps_in, 1, 1))])
@@ -318,7 +336,9 @@
     contract([(z_from, 4 - core * 4, 4) for z_from in ((z + 5) % NZ, z_far, (z + 7) % NZ)])
 
     for way in range(2):
-        wait(ints.at[pl.ds(0, 41), pl.ds(0, 16)], sz.at[way])
+        wait(ints.at[pl.ds(0, 19)], sz.at[way])
+        for side in range(2):
+            wait(ints.at[pl.ds(0, 3), pl.ds(0, 8)], sg.at[way, side])
         wait(ints.at[0], sy.at[way])
         wait(piece(0, 0), sy.at[2 + way])
         wait(ints.at[pl.ds(0, 3), pl.ds(0, 16)], sf.at[way])
@@ -347,11 +367,13 @@
             pltpu.VMEM((4, 24, 128), jnp.int32),
             pltpu.VMEM((1, K), jnp.int32),
             dma((2, 6, 4)),
+            dma((2, 4)),
             dma((3, 2)),
             dma((12,)),
             dma((5, 2)),
             dma((2, 2, 2)),
             dma((3, 2)),
+            dma((2, 2)),
             dma((2,)),
             dma((4,)),
             dma(()),

time: 58.4 us -> 57.9 us (level)
  no operation moved by 1% of the time
where the time goes in v4:
time: 57.9 us; the launch traced here: 57.7 us
  Pallas kernels  56.9 us (98%)
  local copies, waits for them, and re-layouts  0.8 us (1%)
    pallas_call x1, Pallas kernels, on_device(): pl.pallas_call(kernel, out_shape=pltpu.VMEM((ROWS, COLS), F32), in_specs=...  56.9 us

profile of v4, /device:TPU:1, one launch (start us, length us, event | category | flops | bytes accessed | tf_op | source)
XLA Modules:
  0.0 57.7 jit_solution(16408846779778434166)
XLA Ops:
  0.0 56.9 %shard_map.73 = f32[256,512]{1,0:T(8,128)S(1)} custom-call(f32[256,384]{1,0:T(8,128)} %raw.1, f32[32,512]{1,0:T(8,128)} %integ.1, f32[1,256]{1,0:T(1,128)} %bitcast.9, s32[2,256]{1,0:T(2,128)} %bitcast.8, f32[16,128]{1,0:T(8,128)} %bitcast.7, s32[2,3072]{1,0:T(2,128)} %bitcast.5, s32[24,128]{1,0:T(8,128)} %bitcast.6), custom_call_target="tpu_custom_call" | custom-call | tf_op jit(solution)/shard_map/pallas_call | solution.py:354
  56.9 0.8 %copy.9 = f32[256,512]{1,0:T(8,128)} copy(f32[256,512]{1,0:T(8,128)S(1)} %shard_map.73) | data formatting | bytes 1048576

commit v5 on v4

--- a/solution.py
+++ b/solution.py
@@ -319,7 +319,10 @@
     permute(5, 2, [steps((hop, 4, 2)), steps((hop, 4, 3)), steps((far_on,))])
     opposite_in(1)
     scale(7)
-    permute(7, 1, [steps((hop, 5, 1)), steps((hop, 5, 2)), steps((hop, 5, 3))])
+    new = jnp.dot(parts[:, 7 * WIDTH :], pick[7 * WIDTH :, :], preferred_element_type=F32).astype(BF16)
+    moved[...] = moved[...] + new
+    for u in range(1, 4):
+        hop(5, u)
     for i in range(9):
         wait(group(z, 0), rs.at[i])
     out[...] = jnp.zeros_like(out)

time: 57.9 us -> 57.9 us (level)
  no operation moved by 1% of the time
where the time goes in v5:
time: 57.9 us; the launch traced here: 57.7 us
  Pallas kernels  56.9 us (98%)
  local copies, waits for them, and re-layouts  0.8 us (1%)
    pallas_call x1, Pallas kernels, on_device(): pl.pallas_call(kernel, out_shape=pltpu.VMEM((ROWS, COLS), F32), in_specs=...  56.9 us

profile of v5, /device:TPU:1, one launch (start us, length us, event | category | flops | bytes accessed | tf_op | source)
XLA Modules:
  0.0 57.7 jit_solution(4161442354896593822)
XLA Ops:
  0.0 56.9 %shard_map.73 = f32[256,512]{1,0:T(8,128)S(1)} custom-call(f32[256,384]{1,0:T(8,128)} %raw.1, f32[32,512]{1,0:T(8,128)} %integ.1, f32[1,256]{1,0:T(1,128)} %bitcast.9, s32[2,256]{1,0:T(2,128)} %bitcast.8, f32[16,128]{1,0:T(8,128)} %bitcast.7, s32[2,3072]{1,0:T(2,128)} %bitcast.5, s32[24,128]{1,0:T(8,128)} %bitcast.6), custom_call_target="tpu_custom_call" | custom-call | tf_op jit(solution)/shard_map/pallas_call | solution.py:357
  56.9 0.8 %copy.9 = f32[256,512]{1,0:T(8,128)} copy(f32[256,512]{1,0:T(8,128)S(1)} %shard_map.73) | data formatting | bytes 1048576
